TPU v7x, 512 devices: a whole 4x4x16 slice. The times are simulated.
512 devices in a mesh: wide: 128 (over y_hi, x, z), narrow: 4 (over y_lo, core).
Axes of the slice: x: 4, y: 4 (y_hi: 2, y_lo: 2; y = y_hi * 2 + y_lo), z: 16, core: 2. Of those that a mesh axis runs over, the one named last changes fastest.
Arguments:
- treated: bfloat16 [131072, 512], P(('wide', 'narrow')), may hold values from -6 to 6
- control: bfloat16 [131072, 512], P('wide'), may hold values from -6 to 6
- treated_weight: float32 [131072], P(('wide', 'narrow')), may hold values from 0.5 to 2
- control_weight: float32 [131072], replicated, may hold values from 0.5 to 2
- band: int32 [1024, 24], P(('wide', 'narrow')), may hold values from 0 to 1, as said below
Outputs:
- grad_treated: float32 [131072, 512], P(('wide', 'narrow'))
- grad_control: float32 [131072, 512], P(('wide', 'narrow'))
Inputs may be any that keep to these rules, and one draw needn't show every extreme that they name: band[t, k] = 1 pairs treated block t with control block (t // 8 - 1) * 8 + k. For each t the ones form one run of k that contains k = 8 + t % 8; every k whose control block lies outside 0 to 1023 is 0.
All inputs are finite; a program needn't handle non-finite values.
Results may differ from a plain program's by a relative error of at most 0.0055.
Values may be sent and summed in bfloat16 or wider, within the bound.
No kernel may reach another device: no remote copies, remote signals or barrier semaphores. Data moves between devices by JAX's collectives and lax.ppermute only.
A program may use at most 64 MiB of HBM per device.

v0:
```python
import jax
import jax.numpy as jnp
from jax import lax
from jax.sharding import PartitionSpec as P

SWEEPS = 2
SMOOTHING_TEMP = 0.05
EPSILON = 1e-06


def extended(block, sides, width):
    for axis, dim in sides:
        count = lax.axis_size(axis)
        forward = [(i, i + 1) for i in range(count - 1)]
        backward = [(target, source) for source, target in forward]
        low = lax.ppermute(
            lax.slice_in_dim(block, block.shape[dim] - width, None, axis=dim), axis, forward
        )
        high = lax.ppermute(lax.slice_in_dim(block, 0, width, axis=dim), axis, backward)
        block = jnp.concatenate([low, block, high], axis=dim)
    return block


def normalize(features):
    values = features.astype(jnp.float32)
    return (values * lax.rsqrt(jnp.mean(values * values, axis=1, keepdims=True) + EPSILON)).astype(
        jnp.bfloat16
    )


def expand(pair_blocks, block_rows):
    block_count, column_count = pair_blocks.shape
    full = jnp.broadcast_to(
        pair_blocks[:, None, :, None], (block_count, block_rows, column_count, block_rows)
    )
    return full.reshape(block_count * block_rows, column_count * block_rows)


def shards(treated, control, treated_weight, control_weight, band):
    row_count = treated.shape[0]
    slab_rows = control.shape[0]
    feature_total = treated.shape[1]
    block_rows = row_count // band.shape[0]
    wide_index = lax.axis_index("wide")
    narrow_index = lax.axis_index("narrow")
    treated_norm = normalize(treated)
    own_slab = normalize(control)
    band_span = extended(own_slab[None], (("wide", 0),), 1)
    band_span = band_span.reshape(3 * slab_rows, feature_total)
    paired_mask = expand(band, block_rows) > 0
    scale_factor = 1.0 / (feature_total * SMOOTHING_TEMP)
    pairwise_inner = lax.dot_general(
        treated_norm, band_span, (((1,), (1,)), ((), ())), preferred_element_type=jnp.float32
    )
    kernel = jnp.where(paired_mask, jnp.exp(pairwise_inner * scale_factor), 0.0)
    scales = jnp.ones((3 * slab_rows,), jnp.float32)
    own_weight_slab = lax.dynamic_slice_in_dim(control_weight, wide_index * slab_rows, slab_rows)
    row_scale = treated_weight
    for sweep_index in range(SWEEPS):
        row_scale = treated_weight / jnp.sum(kernel * scales[None, :], axis=1)
        column_parts = jnp.sum(kernel * row_scale[:, None], axis=0).reshape(3, slab_rows)
        slab_parts = lax.psum(column_parts, "narrow")
        edges = extended(slab_parts[None], (("wide", 0),), 1)
        column_total = edges[1, 1] + edges[0, 2] + edges[2, 0]
        col_scale = own_weight_slab / column_total
        scales = extended(col_scale[None], (("wide", 0),), 1).reshape(3 * slab_rows)
    transport = row_scale[:, None] * kernel * scales[None, :]
    plan_bf = transport.astype(jnp.bfloat16)
    pulled = jnp.dot(plan_bf, band_span, preferred_element_type=jnp.float32)
    grad_treated = jnp.sum(transport, axis=1)[:, None] * treated_norm.astype(jnp.float32) - pulled
    quarter = slab_rows // lax.axis_size("narrow")
    pushed = lax.dot_general(
        plan_bf, treated_norm, (((0,), (0,)), ((), ())), preferred_element_type=jnp.float32
    )
    pushed = pushed.reshape(3, slab_rows, feature_total)
    neighbours = extended(pushed, (("wide", 0),), 1)
    summed = lax.psum_scatter(
        neighbours[0] + neighbours[2] + neighbours[4], "narrow", scatter_dimension=0, tiled=True
    )
    own_rows = lax.dynamic_slice_in_dim(own_slab, narrow_index * quarter, quarter, 0).astype(
        jnp.float32
    )
    own_weight = lax.dynamic_slice_in_dim(
        control_weight, wide_index * slab_rows + narrow_index * quarter, quarter
    )
    grad_control = own_weight[:, None] * own_rows - summed
    return (grad_treated, grad_control)


def solution(mesh):
    return jax.shard_map(
        shards,
        mesh=mesh,
        in_specs=(
            P(("wide", "narrow"), None),
            P("wide", None),
            P(("wide", "narrow")),
            P(),
            P(("wide", "narrow"), None),
        ),
        out_specs=(P(("wide", "narrow"), None), P(("wide", "narrow"), None)),
        check_vma=False,
    )
```

profile of v0, /device:TPU:1, one launch (start us, length us, event | category | flops | bytes accessed | tf_op | source)
XLA Modules:
  0.0 227.1 jit_solution(4623724721699542760)
XLA Ops:
  7.2 0.0 reduce-scatter.2.cloned.1.call-start
  7.2 1.5 fusion.2
  8.8 1.5 fusion.13
  10.3 1.3 collective-permute-start.1
  11.6 5.1 %collective-permute-start = (bf16[1,1024,512]{2,1,0:T(8,128)(2,1)S(1)}, bf16[1,1024,512]{2,1,0:T(8,128)(2,1)S(1)}, u32[]{:S(2)}, u32[]{:S(2)}) collective-permute-start(bf16[1,1024,512]{2,1,0:T(8,128)(2,1)S(1)} %fusion.13), channel_id=1, source_target_pairs={{0,4},{4,8},{8,12},{12,16},{16,20},{20,24},{24,28},{28,32},{32,36}... | collective-permute-start | bytes 3145736 | tf_op jit(solution)/shard_map/ppermute | solution.py:16
  16.7 0.1 fusion.5
  16.8 15.2 %collective-permute-done.1 = bf16[1,1024,512]{2,1,0:T(8,128)(2,1)S(1)} collective-permute-done((bf16[1,1024,512]{2,1,0:T(8,128)(2,1)S(1)}, bf16[1,1024,512]{2,1,0:T(8,128)(2,1)S(1)}, u32[]{:S(2)}, u32[]{:S(2)}) %collective-permute-start.1) | collective-permute-done | bytes 1048608 | tf_op jit(solution)/shard_map/ppermute | solution.py:19
  32.1 0.9 collective-permute-done
  33.0 0.3 pad_maximum_fusion
  33.3 0.3 broadcast_in_dim.16
  33.6 0.0 copy-start.3
  33.6 1.3 fusion.10
  35.0 0.0 copy-done
  35.0 0.4 multiply_reduce_fusion.1
  35.4 25.4 %psum.14 = f32[1,3,1024]{2,1,0:T(4,128)S(1)} all-reduce(f32[1,3,1024]{2,1,0:T(4,128)S(1)} %broadcast_in_dim.35), channel_id=1, replica_groups=mesh['wide'=128,'narrow'=4] {'narrow'}, use_global_device_ids=true, to_apply=%region_4.5 | all-reduce | flops 3072 | bytes 24576 | tf_op jit(solution)/shard_map/psum | solution.py:62
  60.9 1.3 collective-permute-start.3
  62.2 4.0 %collective-permute-start.2 = (f32[1,3,1024]{2,1,0:T(4,128)S(1)}, f32[1,3,1024]{2,1,0:T(4,128)S(1)}, u32[]{:S(2)}, u32[]{:S(2)}) collective-permute-start(f32[1,3,1024]{2,1,0:T(4,128)S(1)} %psum.14), channel_id=1, source_target_pairs={{0,4},{4,8},{8,12},{12,16},{16,20},{20,24},{24,28},{28,32},{32,36}... | collective-permute-start | bytes 36872 | tf_op jit(solution)/shard_map/ppermute | solution.py:16
  66.2 0.0 collective-permute-done.3
  66.2 0.8 collective-permute-done.2
  67.0 0.7 dynamic-slice_divide_fusion.1
  67.7 1.3 collective-permute-start.5
  69.0 4.3 %collective-permute-start.4 = (f32[1,1024]{1,0:T(1,128)S(1)}, f32[1,1024]{1,0:T(1,128)S(1)}, u32[]{:S(2)}, u32[]{:S(2)}) collective-permute-start(f32[1,1024]{1,0:T(1,128)S(1)} %bitcast.28), channel_id=1, source_target_pairs={{0,4},{4,8},{8,12},{12,16},{16,20},{20,24},{24,28},{28,32},{32,36}... | collective-permute-start | bytes 12296 | tf_op jit(solution)/shard_map/ppermute | solution.py:16
  73.3 0.0 collective-permute-done.5
  73.3 0.7 collective-permute-done.4
  74.0 0.3 multiply_reduce_fusion
  74.4 0.4 multiply_reduce_fusion.3
  74.8 12.4 %psum.15 = f32[1,3,1024]{2,1,0:T(4,128)S(1)} all-reduce(f32[1,3,1024]{2,1,0:T(4,128)S(1)} %broadcast_in_dim.37), channel_id=1, replica_groups=mesh['wide'=128,'narrow'=4] {'narrow'}, use_global_device_ids=true, to_apply=%region_7.8 | all-reduce | flops 3072 | bytes 24576 | tf_op jit(solution)/shard_map/psum | solution.py:62
  87.2 1.3 collective-permute-start.7
  88.5 4.5 %collective-permute-start.6 = (f32[1,3,1024]{2,1,0:T(4,128)S(1)}, f32[1,3,1024]{2,1,0:T(4,128)S(1)}, u32[]{:S(2)}, u32[]{:S(2)}) collective-permute-start(f32[1,3,1024]{2,1,0:T(4,128)S(1)} %psum.15), channel_id=1, source_target_pairs={{0,4},{4,8},{8,12},{12,16},{16,20},{20,24},{24,28},{28,32},{32,36}... | collective-permute-start | bytes 36872 | tf_op jit(solution)/shard_map/ppermute | solution.py:16
  93.1 0.8 collective-permute-done.6
  93.9 0.7 dynamic-slice_divide_fusion
  94.6 1.3 collective-permute-start.9
  95.9 4.3 %collective-permute-start.8 = (f32[1,1024]{1,0:T(1,128)S(1)}, f32[1,1024]{1,0:T(1,128)S(1)}, u32[]{:S(2)}, u32[]{:S(2)}) collective-permute-start(f32[1,1024]{1,0:T(1,128)S(1)} %bitcast.25), channel_id=1, source_target_pairs={{0,4},{4,8},{8,12},{12,16},{16,20},{20,24},{24,28},{28,32},{32,36}... | collective-permute-start | bytes 12296 | tf_op jit(solution)/shard_map/ppermute | solution.py:16
  100.2 0.7 collective-permute-done.8
  101.0 1.1 fusion.7
  102.1 0.4 slice_bitcast_fusion.1
  102.6 1.3 collective-permute-start.11
  103.9 4.4 %collective-permute-start.10 = (f32[1,1024,512]{2,1,0:T(8,128)S(1)}, f32[1,1024,512]{2,1,0:T(8,128)S(1)}, u32[]{:S(2)}, u32[]{:S(2)}) collective-permute-start(f32[1,1024,512]{2,1,0:T(8,128)S(1)} %get-tuple-element.2), channel_id=1, source_target_pairs={{0,4},{4,8},{8,12},{12,16},{16,20},{20,24},{24,28},{28,32},{32,36}... | collective-permute-start | bytes 6291464 | tf_op jit(solution)/shard_map/ppermute | solution.py:16
  108.3 39.4 %collective-permute-done.11 = f32[1,1024,512]{2,1,0:T(8,128)S(1)} collective-permute-done((f32[1,1024,512]{2,1,0:T(8,128)S(1)}, f32[1,1024,512]{2,1,0:T(8,128)S(1)}, u32[]{:S(2)}, u32[]{:S(2)}) %collective-permute-start.11) | collective-permute-done | bytes 2097184 | tf_op jit(solution)/shard_map/ppermute | solution.py:19
  147.7 0.9 collective-permute-done.10
  148.6 2.1 fusion.4
  150.7 0.0 reduce-scatter.2.cloned.1.call-update
  150.7 0.8 dynamic_slice.10
  151.5 2.7 %fusion.3 = bf16[1024,512]{1,0:T(8,128)(2,1)} fusion(bf16[1024,512]{1,0:T(8,128)(2,1)} %param.6, f32[1024]{0:T(1024)S(1)} %add_rsqrt_fusion), kind=kLoop, calls=%fused_computation.12 | loop fusion | flops 1572864 | bytes 2101248 | tf_op jit(solution)/shard_map/convert_element_type | solution.py:26
  154.2 0.5 multiply_reduce_fusion.2
  154.7 1.8 convolution_subtract_fusion
  156.5 61.8 %reduce-scatter.2.cloned.1.call-done = f32[256,512]{1,0:T(8,128)} async-done(((f32[1024,512]{1,0:T(8,128)}), f32[256,512]{1,0:T(8,128)}) %reduce-scatter.2.cloned.1.call-update) | async-done | bytes 524304 | tf_op jit(solution)/shard_map/reduce_scatter | solution.py:77
  218.3 2.0 multiply_subtract_fusion
  (23 shorter events, 0.2 us)
Async XLA Ops:
  7.2 9.5 %copy-start.2 = (bf16[256,512]{1,0:T(8,128)(2,1)S(1)}, bf16[256,512]{1,0:T(8,128)(2,1)}, u32[]{:S(2)}) copy-start(bf16[256,512]{1,0:T(8,128)(2,1)} %param.5) | copy-start | bytes 786436
  7.2 9.6 %copy-start.4 = (s32[2,24]{1,0:T(2,128)S(1)}, s32[2,24]{1,0:T(2,128)}, u32[]{:S(2)}) copy-start(s32[2,24]{1,0:T(2,128)} %param.9) | copy-start | bytes 580
  7.2 211.1 %reduce-scatter.2.cloned.1.call-start = ((), (), s32[]{:S(2)}) async-start(), calls=%async_computation.1 | async-start | bytes 2621440 | tf_op jit(solution)/shard_map/reduce_scatter | solution.py:77
  10.3 21.8 %collective-permute-start.1 = (bf16[1,1024,512]{2,1,0:T(8,128)(2,1)S(1)}, bf16[1,1024,512]{2,1,0:T(8,128)(2,1)S(1)}, u32[]{:S(2)}, u32[]{:S(2)}) collective-permute-start(bf16[1,1024,512]{2,1,0:T(8,128)(2,1)S(1)} %fusion.13), channel_id=1, source_target_pairs={{4,0},{8,4},{12,8},{16,12},{20,16},{24,20},{28,24},{32,28},{36,32}... | collective-permute-start | bytes 3145736 | tf_op jit(solution)/shard_map/ppermute | solution.py:19
  11.6 21.4 %collective-permute-start = (bf16[1,1024,512]{2,1,0:T(8,128)(2,1)S(1)}, bf16[1,1024,512]{2,1,0:T(8,128)(2,1)S(1)}, u32[]{:S(2)}, u32[]{:S(2)}) collective-permute-start(bf16[1,1024,512]{2,1,0:T(8,128)(2,1)S(1)} %fusion.13), channel_id=1, source_target_pairs={{0,4},{4,8},{8,12},{12,16},{16,20},{20,24},{24,28},{28,32},{32,36}... | collective-permute-start | bytes 3145736 | tf_op jit(solution)/shard_map/ppermute | solution.py:16
  33.3 1.7 copy-start
  33.6 1.4 copy-start.3
  60.9 5.3 %collective-permute-start.3 = (f32[1,3,1024]{2,1,0:T(4,128)S(1)}, f32[1,3,1024]{2,1,0:T(4,128)S(1)}, u32[]{:S(2)}, u32[]{:S(2)}) collective-permute-start(f32[1,3,1024]{2,1,0:T(4,128)S(1)} %psum.14), channel_id=1, source_target_pairs={{4,0},{8,4},{12,8},{16,12},{20,16},{24,20},{28,24},{32,28},{36,32}... | collective-permute-start | bytes 36872 | tf_op jit(solution)/shard_map/ppermute | solution.py:19
  62.2 4.8 %collective-permute-start.2 = (f32[1,3,1024]{2,1,0:T(4,128)S(1)}, f32[1,3,1024]{2,1,0:T(4,128)S(1)}, u32[]{:S(2)}, u32[]{:S(2)}) collective-permute-start(f32[1,3,1024]{2,1,0:T(4,128)S(1)} %psum.14), channel_id=1, source_target_pairs={{0,4},{4,8},{8,12},{12,16},{16,20},{20,24},{24,28},{28,32},{32,36}... | collective-permute-start | bytes 36872 | tf_op jit(solution)/shard_map/ppermute | solution.py:16
  67.7 5.6 %collective-permute-start.5 = (f32[1,1024]{1,0:T(1,128)S(1)}, f32[1,1024]{1,0:T(1,128)S(1)}, u32[]{:S(2)}, u32[]{:S(2)}) collective-permute-start(f32[1,1024]{1,0:T(1,128)S(1)} %bitcast.27), channel_id=1, source_target_pairs={{4,0},{8,4},{12,8},{16,12},{20,16},{24,20},{28,24},{32,28},{36,32}... | collective-permute-start | bytes 12296 | tf_op jit(solution)/shard_map/ppermute | solution.py:19
  69.0 5.0 %collective-permute-start.4 = (f32[1,1024]{1,0:T(1,128)S(1)}, f32[1,1024]{1,0:T(1,128)S(1)}, u32[]{:S(2)}, u32[]{:S(2)}) collective-permute-start(f32[1,1024]{1,0:T(1,128)S(1)} %bitcast.28), channel_id=1, source_target_pairs={{0,4},{4,8},{8,12},{12,16},{16,20},{20,24},{24,28},{28,32},{32,36}... | collective-permute-start | bytes 12296 | tf_op jit(solution)/shard_map/ppermute | solution.py:16
  87.2 5.8 %collective-permute-start.7 = (f32[1,3,1024]{2,1,0:T(4,128)S(1)}, f32[1,3,1024]{2,1,0:T(4,128)S(1)}, u32[]{:S(2)}, u32[]{:S(2)}) collective-permute-start(f32[1,3,1024]{2,1,0:T(4,128)S(1)} %psum.15), channel_id=1, source_target_pairs={{4,0},{8,4},{12,8},{16,12},{20,16},{24,20},{28,24},{32,28},{36,32}... | collective-permute-start | bytes 36872 | tf_op jit(solution)/shard_map/ppermute | solution.py:19
  88.5 5.4 %collective-permute-start.6 = (f32[1,3,1024]{2,1,0:T(4,128)S(1)}, f32[1,3,1024]{2,1,0:T(4,128)S(1)}, u32[]{:S(2)}, u32[]{:S(2)}) collective-permute-start(f32[1,3,1024]{2,1,0:T(4,128)S(1)} %psum.15), channel_id=1, source_target_pairs={{0,4},{4,8},{8,12},{12,16},{16,20},{20,24},{24,28},{28,32},{32,36}... | collective-permute-start | bytes 36872 | tf_op jit(solution)/shard_map/ppermute | solution.py:16
  94.6 5.6 %collective-permute-start.9 = (f32[1,1024]{1,0:T(1,128)S(1)}, f32[1,1024]{1,0:T(1,128)S(1)}, u32[]{:S(2)}, u32[]{:S(2)}) collective-permute-start(f32[1,1024]{1,0:T(1,128)S(1)} %bitcast.24), channel_id=1, source_target_pairs={{4,0},{8,4},{12,8},{16,12},{20,16},{24,20},{28,24},{32,28},{36,32}... | collective-permute-start | bytes 12296 | tf_op jit(solution)/shard_map/ppermute | solution.py:19
  95.9 5.0 %collective-permute-start.8 = (f32[1,1024]{1,0:T(1,128)S(1)}, f32[1,1024]{1,0:T(1,128)S(1)}, u32[]{:S(2)}, u32[]{:S(2)}) collective-permute-start(f32[1,1024]{1,0:T(1,128)S(1)} %bitcast.25), channel_id=1, source_target_pairs={{0,4},{4,8},{8,12},{12,16},{16,20},{20,24},{24,28},{28,32},{32,36}... | collective-permute-start | bytes 12296 | tf_op jit(solution)/shard_map/ppermute | solution.py:16
  102.6 45.1 %collective-permute-start.11 = (f32[1,1024,512]{2,1,0:T(8,128)S(1)}, f32[1,1024,512]{2,1,0:T(8,128)S(1)}, u32[]{:S(2)}, u32[]{:S(2)}) collective-permute-start(f32[1,1024,512]{2,1,0:T(8,128)S(1)} %get-tuple-element.3), channel_id=1, source_target_pairs={{4,0},{8,4},{12,8},{16,12},{20,16},{24,20},{28,24},{32,28},{36,32}... | collective-permute-start | bytes 6291464 | tf_op jit(solution)/shard_map/ppermute | solution.py:19
  103.9 44.7 %collective-permute-start.10 = (f32[1,1024,512]{2,1,0:T(8,128)S(1)}, f32[1,1024,512]{2,1,0:T(8,128)S(1)}, u32[]{:S(2)}, u32[]{:S(2)}) collective-permute-start(f32[1,1024,512]{2,1,0:T(8,128)S(1)} %get-tuple-element.2), channel_id=1, source_target_pairs={{0,4},{4,8},{8,12},{12,16},{16,20},{20,24},{24,28},{28,32},{32,36}... | collective-permute-start | bytes 6291464 | tf_op jit(solution)/shard_map/ppermute | solution.py:16
  151.5 3.2 %copy-start.1 = (bf16[3,1024,512]{2,1,0:T(8,128)(2,1)S(1)}, bf16[3,1024,512]{2,1,0:T(8,128)(2,1)}, u32[]{:S(2)}) copy-start(bf16[3,1024,512]{2,1,0:T(8,128)(2,1)} %copy-done) | copy-start | bytes 9437188
Sparse Core Ops, SparseCore 0:
  150.8 67.3 reduce-scatter.1
where the time goes:
time: 228 us; the launch traced here: 227 us
  waiting for transfers between devices  121 us (53%)
  blocking collectives  37.8 us (17%)
  starting transfers between devices  34.2 us (15%)
  between operations  14.3 us (6%)
  other arithmetic  13.5 us (6%)
  matrix products  4.31 us (2%)
    reduce_scatter x1, waiting for transfers between devices, shards(): lax.psum_scatter(neighbours[0] + neighbours[2] + neighbours[4], 'narrow',...  61.8 us
    ppermute x6, waiting for transfers between devices, extended(): lax.ppermute(lax.slice_in_dim(block, 0, width, axis=dim), axis, backward)  54.7 us
    psum x2, blocking collectives, shards(): slab_parts = lax.psum(column_parts, 'narrow')  37.8 us
    ppermute x6, starting transfers between devices, extended(): lax.ppermute(lax.slice_in_dim(block, block.shape[dim] - width, None, axis...  26.5 us
    ppermute x6, starting transfers between devices, extended(): lax.ppermute(lax.slice_in_dim(block, 0, width, axis=dim), axis, backward)  7.71 us
    ppermute x6, waiting for transfers between devices, extended(): lax.ppermute(lax.slice_in_dim(block, block.shape[dim] - width, None, axis...  4.93 us
  transfers between devices with their start and end apart: 13, of which 9 were waited for; matrix products, arithmetic and copies ran while one was open for 3% of the time, Pallas kernels for 0%

commit v1 on v0

--- a/solution.py
+++ b/solution.py
@@ -59,7 +59,8 @@
     for sweep_index in range(SWEEPS):
         row_scale = treated_weight / jnp.sum(kernel * scales[None, :], axis=1)
         column_parts = jnp.sum(kernel * row_scale[:, None], axis=0).reshape(3, slab_rows)
-        slab_parts = lax.psum(column_parts, "narrow")
+        parts = lax.all_gather(column_parts, "narrow")
+        slab_parts = jnp.sum(parts, axis=0)
         edges = extended(slab_parts[None], (("wide", 0),), 1)
         column_total = edges[1, 1] + edges[0, 2] + edges[2, 0]
         col_scale = own_weight_slab / column_total

time: 228 us -> 219 us (0.961)
  blocking collectives: 37.8 us -> 31.7 us
    psum x2 -> x0, blocking collectives: 37.8 us -> none  [shards(): slab_parts = lax.psum(column_parts, 'narrow')]
    all_gather x0 -> x2, blocking collectives: none -> 31.7 us  [shards(): parts = lax.all_gather(column_parts, 'narrow')]
    reduce_scatter x1, waiting for transfers between devices: 61.8 us -> 56.9 us  [shards(): lax.psum_scatter(neighbours[0] + neighbours[2] + neighbours[4], 'narrow',...]
where the time goes in v1:
time: 219 us; the launch traced here: 218 us
  waiting for transfers between devices  119 us (54%)
  starting transfers between devices  34.4 us (16%)
  blocking collectives  31.7 us (14%)
  between operations  14.3 us (7%)
  other arithmetic  13.5 us (6%)
  matrix products  4.31 us (2%)
    ppermute x6, waiting for transfers between devices, extended(): lax.ppermute(lax.slice_in_dim(block, 0, width, axis=dim), axis, backward)  56.9 us
    reduce_scatter x1, waiting for transfers between devices, shards(): lax.psum_scatter(neighbours[0] + neighbours[2] + neighbours[4], 'narrow',...  56.9 us
    all_gather x2, blocking collectives, shards(): parts = lax.all_gather(column_parts, 'narrow')  31.7 us
    ppermute x6, starting transfers between devices, extended(): lax.ppermute(lax.slice_in_dim(block, block.shape[dim] - width, None, axis...  26.6 us
    ppermute x6, starting transfers between devices, extended(): lax.ppermute(lax.slice_in_dim(block, 0, width, axis=dim), axis, backward)  7.74 us
    ppermute x6, waiting for transfers between devices, extended(): lax.ppermute(lax.slice_in_dim(block, block.shape[dim] - width, None, axis...  4.93 us
  transfers between devices with their start and end apart: 13, of which 9 were waited for; matrix products, arithmetic and copies ran while one was open for 3% of the time, Pallas kernels for 0%

profile of v1, /device:TPU:1, one launch (start us, length us, event | category | flops | bytes accessed | tf_op | source)
XLA Modules:
  0.0 218.5 jit_solution(2672861399812301955)
XLA Ops:
  7.2 0.0 reduce-scatter.2.cloned.1.call-start
  7.2 1.5 fusion.2
  8.8 1.5 fusion.13
  10.3 1.3 collective-permute-start.1
  11.6 5.1 %collective-permute-start = (bf16[1,1024,512]{2,1,0:T(8,128)(2,1)S(1)}, bf16[1,1024,512]{2,1,0:T(8,128)(2,1)S(1)}, u32[]{:S(2)}, u32[]{:S(2)}) collective-permute-start(bf16[1,1024,512]{2,1,0:T(8,128)(2,1)S(1)} %fusion.13), channel_id=1, source_target_pairs={{0,4},{4,8},{8,12},{12,16},{16,20},{20,24},{24,28},{28,32},{32,36}... | collective-permute-start | bytes 3145736 | tf_op jit(solution)/shard_map/ppermute | solution.py:16
  16.7 0.1 fusion.5
  16.8 15.2 %collective-permute-done.1 = bf16[1,1024,512]{2,1,0:T(8,128)(2,1)S(1)} collective-permute-done((bf16[1,1024,512]{2,1,0:T(8,128)(2,1)S(1)}, bf16[1,1024,512]{2,1,0:T(8,128)(2,1)S(1)}, u32[]{:S(2)}, u32[]{:S(2)}) %collective-permute-start.1) | collective-permute-done | bytes 1048608 | tf_op jit(solution)/shard_map/ppermute | solution.py:19
  32.1 0.9 collective-permute-done
  33.0 0.3 pad_maximum_fusion
  33.3 0.3 broadcast_in_dim.16
  33.6 0.0 copy-start.3
  33.6 1.3 fusion.10
  35.0 0.0 copy-done
  35.0 0.4 multiply_reduce_fusion.1
  35.4 24.2 %all_gather.6 = f32[4,3,1024]{2,1,0:T(4,128)S(1)} all-gather(f32[1,3,1024]{2,1,0:T(4,128)S(1)} %all_gather_reshape.6), channel_id=1, replica_groups=mesh['wide'=128,'narrow'=4] {'narrow'}, dimensions={0}, use_global_device_ids=true | all-gather | bytes 61440 | tf_op jit(solution)/shard_map/all_gather | solution.py:62
  59.7 1.3 collective-permute-start.3
  61.0 4.0 %collective-permute-start.2 = (f32[1,3,1024]{2,1,0:T(4,128)S(1)}, f32[1,3,1024]{2,1,0:T(4,128)S(1)}, u32[]{:S(2)}, u32[]{:S(2)}) collective-permute-start(f32[1,3,1024]{2,1,0:T(4,128)S(1)} %bitcast.27), channel_id=1, source_target_pairs={{0,4},{4,8},{8,12},{12,16},{16,20},{20,24},{24,28},{28,32},{32,36}... | collective-permute-start | bytes 36872 | tf_op jit(solution)/shard_map/ppermute | solution.py:16
  65.0 0.0 collective-permute-done.3
  65.0 0.8 collective-permute-done.2
  65.8 0.7 dynamic-slice_divide_fusion.1
  66.5 1.3 collective-permute-start.5
  67.8 4.3 %collective-permute-start.4 = (f32[1,1024]{1,0:T(1,128)S(1)}, f32[1,1024]{1,0:T(1,128)S(1)}, u32[]{:S(2)}, u32[]{:S(2)}) collective-permute-start(f32[1,1024]{1,0:T(1,128)S(1)} %bitcast.36), channel_id=1, source_target_pairs={{0,4},{4,8},{8,12},{12,16},{16,20},{20,24},{24,28},{28,32},{32,36}... | collective-permute-start | bytes 12296 | tf_op jit(solution)/shard_map/ppermute | solution.py:16
  72.1 0.7 collective-permute-done.4
  72.9 0.3 multiply_reduce_fusion
  73.2 0.4 multiply_reduce_fusion.3
  73.6 7.5 %all_gather.7 = f32[4,3,1024]{2,1,0:T(4,128)S(1)} all-gather(f32[1,3,1024]{2,1,0:T(4,128)S(1)} %all_gather_reshape.7), channel_id=1, replica_groups=mesh['wide'=128,'narrow'=4] {'narrow'}, dimensions={0}, use_global_device_ids=true | all-gather | bytes 61440 | tf_op jit(solution)/shard_map/all_gather | solution.py:62
  81.2 1.3 collective-permute-start.7
  82.5 4.5 %collective-permute-start.6 = (f32[1,3,1024]{2,1,0:T(4,128)S(1)}, f32[1,3,1024]{2,1,0:T(4,128)S(1)}, u32[]{:S(2)}, u32[]{:S(2)}) collective-permute-start(f32[1,3,1024]{2,1,0:T(4,128)S(1)} %bitcast.30), channel_id=1, source_target_pairs={{0,4},{4,8},{8,12},{12,16},{16,20},{20,24},{24,28},{28,32},{32,36}... | collective-permute-start | bytes 36872 | tf_op jit(solution)/shard_map/ppermute | solution.py:16
  87.0 0.8 collective-permute-done.6
  87.9 0.7 dynamic-slice_divide_fusion
  88.6 1.3 collective-permute-start.9
  89.9 4.3 %collective-permute-start.8 = (f32[1,1024]{1,0:T(1,128)S(1)}, f32[1,1024]{1,0:T(1,128)S(1)}, u32[]{:S(2)}, u32[]{:S(2)}) collective-permute-start(f32[1,1024]{1,0:T(1,128)S(1)} %bitcast.33), channel_id=1, source_target_pairs={{0,4},{4,8},{8,12},{12,16},{16,20},{20,24},{24,28},{28,32},{32,36}... | collective-permute-start | bytes 12296 | tf_op jit(solution)/shard_map/ppermute | solution.py:16
  94.2 0.0 collective-permute-done.9
  94.2 0.7 collective-permute-done.8
  94.9 1.1 fusion.7
  96.1 0.4 slice_bitcast_fusion.1
  96.5 1.3 collective-permute-start.11
  97.8 4.5 %collective-permute-start.10 = (f32[1,1024,512]{2,1,0:T(8,128)S(1)}, f32[1,1024,512]{2,1,0:T(8,128)S(1)}, u32[]{:S(2)}, u32[]{:S(2)}) collective-permute-start(f32[1,1024,512]{2,1,0:T(8,128)S(1)} %get-tuple-element.2), channel_id=1, source_target_pairs={{0,4},{4,8},{8,12},{12,16},{16,20},{20,24},{24,28},{28,32},{32,36}... | collective-permute-start | bytes 6291464 | tf_op jit(solution)/shard_map/ppermute | solution.py:16
  102.3 41.6 %collective-permute-done.11 = f32[1,1024,512]{2,1,0:T(8,128)S(1)} collective-permute-done((f32[1,1024,512]{2,1,0:T(8,128)S(1)}, f32[1,1024,512]{2,1,0:T(8,128)S(1)}, u32[]{:S(2)}, u32[]{:S(2)}) %collective-permute-start.11) | collective-permute-done | bytes 2097184 | tf_op jit(solution)/shard_map/ppermute | solution.py:19
  143.9 0.9 collective-permute-done.10
  144.8 2.1 fusion.4
  147.0 0.0 reduce-scatter.2.cloned.1.call-update
  147.0 0.8 dynamic_slice.10
  147.8 2.7 %fusion.3 = bf16[1024,512]{1,0:T(8,128)(2,1)} fusion(bf16[1024,512]{1,0:T(8,128)(2,1)} %param.6, f32[1024]{0:T(1024)S(1)} %add_rsqrt_fusion), kind=kLoop, calls=%fused_computation.12 | loop fusion | flops 1572864 | bytes 2101248 | tf_op jit(solution)/shard_map/convert_element_type | solution.py:26
  150.4 0.5 multiply_reduce_fusion.2
  150.9 1.8 convolution_subtract_fusion
  152.7 56.9 %reduce-scatter.2.cloned.1.call-done = f32[256,512]{1,0:T(8,128)} async-done(((f32[1024,512]{1,0:T(8,128)}), f32[256,512]{1,0:T(8,128)}) %reduce-scatter.2.cloned.1.call-update) | async-done | bytes 524304 | tf_op jit(solution)/shard_map/reduce_scatter | solution.py:78
  209.6 2.0 multiply_subtract_fusion
  (25 shorter events, 0.2 us)
Async XLA Ops:
  7.2 9.5 %copy-start.2 = (bf16[256,512]{1,0:T(8,128)(2,1)S(1)}, bf16[256,512]{1,0:T(8,128)(2,1)}, u32[]{:S(2)}) copy-start(bf16[256,512]{1,0:T(8,128)(2,1)} %param.5) | copy-start | bytes 786436
  7.2 9.6 %copy-start.4 = (s32[2,24]{1,0:T(2,128)S(1)}, s32[2,24]{1,0:T(2,128)}, u32[]{:S(2)}) copy-start(s32[2,24]{1,0:T(2,128)} %param.9) | copy-start | bytes 580
  7.2 202.4 %reduce-scatter.2.cloned.1.call-start = ((), (), s32[]{:S(2)}) async-start(), calls=%async_computation.1 | async-start | bytes 2621440 | tf_op jit(solution)/shard_map/reduce_scatter | solution.py:78
  10.3 21.8 %collective-permute-start.1 = (bf16[1,1024,512]{2,1,0:T(8,128)(2,1)S(1)}, bf16[1,1024,512]{2,1,0:T(8,128)(2,1)S(1)}, u32[]{:S(2)}, u32[]{:S(2)}) collective-permute-start(bf16[1,1024,512]{2,1,0:T(8,128)(2,1)S(1)} %fusion.13), channel_id=1, source_target_pairs={{4,0},{8,4},{12,8},{16,12},{20,16},{24,20},{28,24},{32,28},{36,32}... | collective-permute-start | bytes 3145736 | tf_op jit(solution)/shard_map/ppermute | solution.py:19
  11.6 21.4 %collective-permute-start = (bf16[1,1024,512]{2,1,0:T(8,128)(2,1)S(1)}, bf16[1,1024,512]{2,1,0:T(8,128)(2,1)S(1)}, u32[]{:S(2)}, u32[]{:S(2)}) collective-permute-start(bf16[1,1024,512]{2,1,0:T(8,128)(2,1)S(1)} %fusion.13), channel_id=1, source_target_pairs={{0,4},{4,8},{8,12},{12,16},{16,20},{20,24},{24,28},{28,32},{32,36}... | collective-permute-start | bytes 3145736 | tf_op jit(solution)/shard_map/ppermute | solution.py:16
  33.3 1.7 copy-start
  33.6 1.4 copy-start.3
  59.7 5.3 %collective-permute-start.3 = (f32[1,3,1024]{2,1,0:T(4,128)S(1)}, f32[1,3,1024]{2,1,0:T(4,128)S(1)}, u32[]{:S(2)}, u32[]{:S(2)}) collective-permute-start(f32[1,3,1024]{2,1,0:T(4,128)S(1)} %bitcast.26), channel_id=1, source_target_pairs={{4,0},{8,4},{12,8},{16,12},{20,16},{24,20},{28,24},{32,28},{36,32}... | collective-permute-start | bytes 36872 | tf_op jit(solution)/shard_map/ppermute | solution.py:19
  61.0 4.8 %collective-permute-start.2 = (f32[1,3,1024]{2,1,0:T(4,128)S(1)}, f32[1,3,1024]{2,1,0:T(4,128)S(1)}, u32[]{:S(2)}, u32[]{:S(2)}) collective-permute-start(f32[1,3,1024]{2,1,0:T(4,128)S(1)} %bitcast.27), channel_id=1, source_target_pairs={{0,4},{4,8},{8,12},{12,16},{16,20},{20,24},{24,28},{28,32},{32,36}... | collective-permute-start | bytes 36872 | tf_op jit(solution)/shard_map/ppermute | solution.py:16
  66.5 5.6 %collective-permute-start.5 = (f32[1,1024]{1,0:T(1,128)S(1)}, f32[1,1024]{1,0:T(1,128)S(1)}, u32[]{:S(2)}, u32[]{:S(2)}) collective-permute-start(f32[1,1024]{1,0:T(1,128)S(1)} %bitcast.35), channel_id=1, source_target_pairs={{4,0},{8,4},{12,8},{16,12},{20,16},{24,20},{28,24},{32,28},{36,32}... | collective-permute-start | bytes 12296 | tf_op jit(solution)/shard_map/ppermute | solution.py:19
  67.8 5.0 %collective-permute-start.4 = (f32[1,1024]{1,0:T(1,128)S(1)}, f32[1,1024]{1,0:T(1,128)S(1)}, u32[]{:S(2)}, u32[]{:S(2)}) collective-permute-start(f32[1,1024]{1,0:T(1,128)S(1)} %bitcast.36), channel_id=1, source_target_pairs={{0,4},{4,8},{8,12},{12,16},{16,20},{20,24},{24,28},{28,32},{32,36}... | collective-permute-start | bytes 12296 | tf_op jit(solution)/shard_map/ppermute | solution.py:16
  81.2 5.8 %collective-permute-start.7 = (f32[1,3,1024]{2,1,0:T(4,128)S(1)}, f32[1,3,1024]{2,1,0:T(4,128)S(1)}, u32[]{:S(2)}, u32[]{:S(2)}) collective-permute-start(f32[1,3,1024]{2,1,0:T(4,128)S(1)} %bitcast.29), channel_id=1, source_target_pairs={{4,0},{8,4},{12,8},{16,12},{20,16},{24,20},{28,24},{32,28},{36,32}... | collective-permute-start | bytes 36872 | tf_op jit(solution)/shard_map/ppermute | solution.py:19
  82.5 5.4 %collective-permute-start.6 = (f32[1,3,1024]{2,1,0:T(4,128)S(1)}, f32[1,3,1024]{2,1,0:T(4,128)S(1)}, u32[]{:S(2)}, u32[]{:S(2)}) collective-permute-start(f32[1,3,1024]{2,1,0:T(4,128)S(1)} %bitcast.30), channel_id=1, source_target_pairs={{0,4},{4,8},{8,12},{12,16},{16,20},{20,24},{24,28},{28,32},{32,36}... | collective-permute-start | bytes 36872 | tf_op jit(solution)/shard_map/ppermute | solution.py:16
  88.6 5.6 %collective-permute-start.9 = (f32[1,1024]{1,0:T(1,128)S(1)}, f32[1,1024]{1,0:T(1,128)S(1)}, u32[]{:S(2)}, u32[]{:S(2)}) collective-permute-start(f32[1,1024]{1,0:T(1,128)S(1)} %bitcast.32), channel_id=1, source_target_pairs={{4,0},{8,4},{12,8},{16,12},{20,16},{24,20},{28,24},{32,28},{36,32}... | collective-permute-start | bytes 12296 | tf_op jit(solution)/shard_map/ppermute | solution.py:19
  89.9 5.0 %collective-permute-start.8 = (f32[1,1024]{1,0:T(1,128)S(1)}, f32[1,1024]{1,0:T(1,128)S(1)}, u32[]{:S(2)}, u32[]{:S(2)}) collective-permute-start(f32[1,1024]{1,0:T(1,128)S(1)} %bitcast.33), channel_id=1, source_target_pairs={{0,4},{4,8},{8,12},{12,16},{16,20},{20,24},{24,28},{28,32},{32,36}... | collective-permute-start | bytes 12296 | tf_op jit(solution)/shard_map/ppermute | solution.py:16
  96.5 47.4 %collective-permute-start.11 = (f32[1,1024,512]{2,1,0:T(8,128)S(1)}, f32[1,1024,512]{2,1,0:T(8,128)S(1)}, u32[]{:S(2)}, u32[]{:S(2)}) collective-permute-start(f32[1,1024,512]{2,1,0:T(8,128)S(1)} %get-tuple-element.3), channel_id=1, source_target_pairs={{4,0},{8,4},{12,8},{16,12},{20,16},{24,20},{28,24},{32,28},{36,32}... | collective-permute-start | bytes 6291464 | tf_op jit(solution)/shard_map/ppermute | solution.py:19
  97.8 47.0 %collective-permute-start.10 = (f32[1,1024,512]{2,1,0:T(8,128)S(1)}, f32[1,1024,512]{2,1,0:T(8,128)S(1)}, u32[]{:S(2)}, u32[]{:S(2)}) collective-permute-start(f32[1,1024,512]{2,1,0:T(8,128)S(1)} %get-tuple-element.2), channel_id=1, source_target_pairs={{0,4},{4,8},{8,12},{12,16},{16,20},{20,24},{24,28},{28,32},{32,36}... | collective-permute-start | bytes 6291464 | tf_op jit(solution)/shard_map/ppermute | solution.py:16
  147.8 3.2 %copy-start.1 = (bf16[3,1024,512]{2,1,0:T(8,128)(2,1)S(1)}, bf16[3,1024,512]{2,1,0:T(8,128)(2,1)}, u32[]{:S(2)}) copy-start(bf16[3,1024,512]{2,1,0:T(8,128)(2,1)} %copy-done) | copy-start | bytes 9437188
Sparse Core Ops, SparseCore 0:
  147.1 62.4 reduce-scatter.1
